TPU v7x, 256 devices: a whole 4x4x8 slice. The times are simulated.
256 devices in a mesh: row: 4 (over x_hi, core), col: 8 (over z), layer: 8 (over x_lo, y).
Axes of the slice: x: 4 (x_hi: 2, x_lo: 2; x = x_hi * 2 + x_lo), y: 4, z: 8, core: 2. Of those that a mesh axis runs over, the one named last changes fastest.
Arguments:
- amplitudes: float32 [12288, 16384], P(('row', 'col', 'layer')), may hold values from -6 to 6
- integrals: float32 [16384, 2048], P(('col', 'layer')), may hold values from -0.046875 to 0.046875
- pair_list: int32 [12288, 2], P(('row', 'col', 'layer')), may hold values from 0 to 199, as said below
- occupied_energy: float32 [200], replicated, may hold values from -1.5 to -0.3
- virtual_energy: float32 [2048], replicated, may hold values from 1 to 4
Outputs:
- ladder_update: float32 [12288, 2048], P(('row', 'col', 'layer'))
Inputs may be any that keep to these rules, and one draw needn't show every extreme that they name: `pair_list`: each row (i, j) holds two occupied orbital numbers with i <= j.
All inputs are finite; a program needn't handle non-finite values.
Results may differ from a plain program's by a relative error of at most 0.000071.
Values sent between devices are 32-bit elements; how exact they have to be, the bound alone decides.
No kernel may reach another device: no remote copies, remote signals or barrier semaphores. Data moves between devices by JAX's collectives and lax.ppermute only.
A program may use at most 128 MiB of HBM per device.

v0:
```python
import jax
import jax.numpy as jnp
from jax import lax
from jax.sharding import PartitionSpec as P


def energy_lookup(pair_list, occupied_energy):
    occ_index = jnp.arange(occupied_energy.shape[0], dtype=jnp.int32)
    occ_first = jnp.sum(
        jnp.where(pair_list[:, 0:1] == occ_index[None, :], occupied_energy[None, :], 0.0), axis=1
    )
    occ_second = jnp.sum(
        jnp.where(pair_list[:, 1:2] == occ_index[None, :], occupied_energy[None, :], 0.0), axis=1
    )
    return (occ_first, occ_second)


def body(amplitudes, integrals, pair_list, occupied_energy, virtual_energy):
    row_count = amplitudes.shape[0]
    col_count = lax.axis_size("col")
    integral_block = lax.all_gather(integrals, "layer", axis=0, tiled=True)
    shaped = amplitudes.reshape(row_count, col_count, amplitudes.shape[1] // col_count)
    partial_value = jnp.einsum(
        "rsk,kn->rsn",
        lax.all_to_all(shaped, "col", split_axis=1, concat_axis=1, tiled=True),
        integral_block,
        precision=lax.Precision.HIGHEST,
        preferred_element_type=jnp.float32,
    )
    returned = lax.all_to_all(partial_value, "col", split_axis=1, concat_axis=1, tiled=True)
    ladder = jnp.sum(returned, axis=1)
    occ_first, occ_second = energy_lookup(pair_list, occupied_energy)
    denominator = virtual_energy[None, :] - occ_first[:, None] - occ_second[:, None]
    return ladder / denominator


def solution(mesh):
    in_specs = (
        P(("row", "col", "layer"), None),
        P(("col", "layer"), None),
        P(("row", "col", "layer"), None),
        P(),
        P(),
    )
    out_specs = P(("row", "col", "layer"), None)
    return jax.shard_map(body, mesh=mesh, in_specs=in_specs, out_specs=out_specs, check_vma=False)
```

profile of v0, /device:TPU:1, one launch (start us, length us, event | category | flops | bytes accessed | tf_op | source)
XLA Modules:
  0.0 299.0 jit_solution(12691873429440723505)
XLA Ops:
  6.5 0.0 all-gather.2.cloned.1.call-start
  6.5 0.7 all-gather.2.cloned.1.call-update
  7.3 2.1 copy.18
  9.4 81.1 %all_to_all.10 = f32[48,8,2048]{2,0,1:T(8,128)S(1)} all-to-all(f32[48,8,2048]{2,0,1:T(8,128)S(1)} %bitcast.12), channel_id=1, replica_groups=mesh['row'=4,'col'=8,'layer'=8] {'col'}, dimensions={1} | all-to-all | bytes 6291456 | tf_op jit(solution)/shard_map/all_to_all | solution.py:25
  90.4 95.4 %all-gather.2.cloned.1.call-done = f32[2048,2048]{1,0:T(8,128)} async-done(((f32[256,2048]{1,0:T(8,128)}), f32[2048,2048]{1,0:T(8,128)}) %all-gather.2.cloned.1.call-update) | async-done | bytes 16777232 | tf_op jit(solution)/shard_map/all_gather | solution.py:21
  185.8 24.1 %fusion = f32[48,8,2048]{2,0,1:T(8,128)} fusion(f32[48,8,2048]{2,0,1:T(8,128)S(1)} %all_to_all.10, f32[2048,2048]{1,0:T(8,128)} %all-gather.2.cloned.1.call-done), kind=kOutput, calls=%fused_computation | convolution fusion | flops 19327352832 | bytes 23068672 | tf_op jit(solution)/shard_map/rsk,kn->rsn/dot_general | solution.py:23
  209.9 0.0 copy-start.2
  209.9 0.0 copy-start.1
  209.9 6.9 %all-to-all-start.1 = ((f32[48,8,2048]{2,0,1:T(8,128)}), f32[48,8,2048]{2,0,1:T(8,128)S(1)}, u32[]{:S(2)}, u32[]{:S(2)}) async-start(f32[48,8,2048]{2,0,1:T(8,128)} %fusion), calls=%async_computation.1 | async-start | bytes 6291456 | tf_op jit(solution)/shard_map/all_to_all | solution.py:30
  216.8 0.0 copy-done.2
  216.8 0.0 copy-start
  216.9 0.0 copy-done.1
  216.9 0.2 select_reduce_fusion.1
  217.0 74.0 %all-to-all-done.1 = f32[48,8,2048]{2,0,1:T(8,128)S(1)} async-done(((f32[48,8,2048]{2,0,1:T(8,128)}), f32[48,8,2048]{2,0,1:T(8,128)S(1)}, u32[]{:S(2)}, u32[]{:S(2)}) %all-to-all-start.1) | async-done | bytes 3145760 | tf_op jit(solution)/shard_map/all_to_all | solution.py:30
  291.1 0.2 reduce_sum.27
  291.3 0.0 copy-done
  291.3 0.9 subtract_divide_fusion
  (1 shorter events, 0.0 us)
Async XLA Ops:
  6.5 179.3 %all-gather.2.cloned.1.call-start = ((), (), s32[]{:S(2)}) async-start(), calls=%async_computation.2 | async-start | bytes 18874368 | tf_op jit(solution)/shard_map/all_gather | solution.py:21
  209.9 6.9 %copy-start.2 = (s32[48,2]{0,1:T(2,128)S(1)}, s32[48,2]{0,1:T(2,128)}, u32[]{:S(2)}) copy-start(s32[48,2]{0,1:T(2,128)} %param.7) | copy-start | bytes 1156
  209.9 6.9 %copy-start.1 = (f32[200]{0:T(256)S(1)}, f32[200]{0:T(256)}, u32[]{:S(2)}) copy-start(f32[200]{0:T(256)} %param.8) | copy-start | bytes 2404
  209.9 81.1 %all-to-all-start.1 = ((f32[48,8,2048]{2,0,1:T(8,128)}), f32[48,8,2048]{2,0,1:T(8,128)S(1)}, u32[]{:S(2)}, u32[]{:S(2)}) async-start(f32[48,8,2048]{2,0,1:T(8,128)} %fusion), calls=%async_computation.1 | async-start | bytes 6291456 | tf_op jit(solution)/shard_map/all_to_all | solution.py:30
  216.8 74.4 %copy-start = (f32[2048]{0:T(1024)S(1)}, f32[2048]{0:T(1024)}, u32[]{:S(2)}) copy-start(f32[2048]{0:T(1024)} %param.9) | copy-start | bytes 24580
Sparse Core Ops, SparseCore 0:
  9.1 176.6 all-gather.1
where the time goes:
time: 299 us
  waiting for transfers between devices  170 us (57%)
  blocking collectives  81.1 us (27%)
  matrix products  24.1 us (8%)
  between operations  13.4 us (4%)
  starting transfers between devices  6.88 us (2%)
    all_gather x1, waiting for transfers between devices, body(): integral_block = lax.all_gather(integrals, 'layer', axis=0, tiled=True)  95.4 us
    all_to_all x1, blocking collectives, body(): lax.all_to_all(shaped, 'col', split_axis=1, concat_axis=1, tiled=True)  81.1 us
    all_to_all x1, waiting for transfers between devices, body(): lax.all_to_all(partial_value, 'col', split_axis=1, concat_axis=1, tiled=T...  74 us
    dot_general x1, matrix products, body(): jnp.einsum('rsk,kn->rsn', lax.all_to_all(shaped, 'col', split_axis=1, con...  24.1 us
    all_to_all x1, starting transfers between devices, body(): lax.all_to_all(partial_value, 'col', split_axis=1, concat_axis=1, tiled=T...  6.88 us
  transfers between devices with their start and end apart: 2, of which 2 were waited for; matrix products, arithmetic and copies ran while one was open for 1% of the time, Pallas kernels for 0%

commit v1 on v0

--- a/solution.py
+++ b/solution.py
@@ -18,7 +18,9 @@
 def body(amplitudes, integrals, pair_list, occupied_energy, virtual_energy):
     row_count = amplitudes.shape[0]
     col_count = lax.axis_size("col")
-    integral_block = lax.all_gather(integrals, "layer", axis=0, tiled=True)
+    integral_block = jnp.concatenate(
+        lax.all_to_all(jnp.stack([integrals] * lax.axis_size("layer")), "layer", 0, 0), axis=0
+    )
     shaped = amplitudes.reshape(row_count, col_count, amplitudes.shape[1] // col_count)
     partial_value = jnp.einsum(
         "rsk,kn->rsn",

time: 299 us -> 379 us (1.27); the launches traced: 299 us -> 375 us
  blocking collectives: 81.1 us -> 267 us
  waiting for transfers between devices: 170 us -> 69.8 us
  between operations: 13.4 us -> 0.06 us
  local copies, waits for them, and re-layouts: 2.11 us -> 9.95 us
    all_to_all x0 -> x1, blocking collectives: none -> 186 us  [body(): lax.all_to_all(jnp.stack([integrals] * lax.axis_size('layer')), 'layer',...]
    all_gather x1 -> x0, waiting for transfers between devices: 95.4 us -> none  [body(): integral_block = lax.all_gather(integrals, 'layer', axis=0, tiled=True)]
    another operation x0 -> x1, local copies, waits for them, and re-layouts: none -> 7.84 us  [body(): jnp.stack([integrals] * lax.axis_size('layer'))]
    all_to_all x1, waiting for transfers between devices: 74 us -> 69.8 us  [body(): lax.all_to_all(partial_value, 'col', split_axis=1, concat_axis=1, tiled=T...]
  transfers between devices with their start and end apart: 2 -> 1, of which waited for: 2 -> 1; matrix products, arithmetic and copies ran while one was open for 1% -> 0% of each run, Pallas kernels for 0% -> 0%
where the time goes in v1:
time: 379 us; the launch traced here: 375 us
  blocking collectives  267 us (70%)
  waiting for transfers between devices  69.8 us (18%)
  matrix products  22.1 us (6%)
  local copies, waits for them, and re-layouts  9.95 us (3%)
  starting transfers between devices  4 us (1%)
    all_to_all x1, blocking collectives, body(): lax.all_to_all(jnp.stack([integrals] * lax.axis_size('layer')), 'layer',...  186 us
    all_to_all x1, blocking collectives, body(): lax.all_to_all(shaped, 'col', split_axis=1, concat_axis=1, tiled=True)  81.2 us
    all_to_all x1, waiting for transfers between devices, body(): lax.all_to_all(partial_value, 'col', split_axis=1, concat_axis=1, tiled=T...  69.8 us
    dot_general x1, matrix products, body(): jnp.einsum('rsk,kn->rsn', lax.all_to_all(shaped, 'col', split_axis=1, con...  22.1 us
    another operation x1, local copies, waits for them, and re-layouts, body(): jnp.stack([integrals] * lax.axis_size('layer'))  7.84 us
  transfers between devices with their start and end apart: 1, of which 1 were waited for; matrix products, arithmetic and copies ran while one was open for 0% of the time, Pallas kernels for 0%

profile of v1, /device:TPU:1, one launch (start us, length us, event | category | flops | bytes accessed | tf_op | source)
XLA Modules:
  0.0 374.6 jit_solution(3521370260746397364)
XLA Ops:
  0.0 2.1 copy.18
  2.1 0.0 copy-start
  2.1 81.2 %all_to_all.15 = f32[48,8,2048]{2,0,1:T(8,128)S(1)} all-to-all(f32[48,8,2048]{2,0,1:T(8,128)S(1)} %bitcast.14), channel_id=1, replica_groups=mesh['row'=4,'col'=8,'layer'=8] {'col'}, dimensions={1} | all-to-all | bytes 6291456 | tf_op jit(solution)/shard_map/all_to_all | solution.py:27
  83.3 0.0 copy-done
  83.3 7.8 %stack.2 = f32[8,256,2048]{2,1,0:T(8,128)} broadcast(f32[256,2048]{1,0:T(8,128)S(1)} %copy-done), dimensions={1,2} | broadcast | bytes 18874368 | tf_op jit(solution)/shard_map/stack | solution.py:22
  91.2 186.2 %all_to_all.16 = f32[8,256,2048]{2,1,0:T(8,128)S(1)} all-to-all(f32[8,256,2048]{2,1,0:T(8,128)} %stack.2), channel_id=1, replica_groups=mesh['row'=4,'col'=8,'layer'=8] {'layer'}, dimensions={0} | all-to-all | bytes 33554432 | tf_op jit(solution)/shard_map/all_to_all | solution.py:22
  277.3 22.1 %fusion = f32[48,8,2048]{2,0,1:T(8,128)} fusion(f32[48,8,2048]{2,0,1:T(8,128)S(1)} %all_to_all.15, f32[2048,2048,1]{1,0,2:T(8,128)S(1)} %bitcast.13), kind=kOutput, calls=%fused_computation.8 | convolution fusion | flops 19327352832 | bytes 23068672 | tf_op jit(solution)/shard_map/rsk,kn->rsn/dot_general | solution.py:25
  299.5 0.0 copy-start.3
  299.5 0.0 copy-start.2
  299.5 4.0 %all-to-all-start.2 = ((f32[48,8,2048]{2,0,1:T(8,128)}), f32[48,8,2048]{2,0,1:T(8,128)S(1)}, u32[]{:S(2)}, u32[]{:S(2)}) async-start(f32[48,8,2048]{2,0,1:T(8,128)} %fusion), calls=%async_computation.2 | async-start | bytes 6291456 | tf_op jit(solution)/shard_map/all_to_all | solution.py:32
  303.5 0.0 copy-done.3
  303.5 0.0 copy-start.1
  303.5 0.0 copy-done.2
  303.5 0.2 select_reduce_fusion.1
  303.7 69.8 %all-to-all-done.2 = f32[48,8,2048]{2,0,1:T(8,128)S(1)} async-done(((f32[48,8,2048]{2,0,1:T(8,128)}), f32[48,8,2048]{2,0,1:T(8,128)S(1)}, u32[]{:S(2)}, u32[]{:S(2)}) %all-to-all-start.2) | async-done | bytes 3145760 | tf_op jit(solution)/shard_map/all_to_all | solution.py:32
  373.5 0.2 reduce_sum.27
  373.7 0.0 copy-done.1
  373.7 0.9 subtract_divide_fusion
  (1 shorter events, 0.0 us)
Async XLA Ops:
  2.1 81.2 %copy-start = (f32[256,2048]{1,0:T(8,128)S(1)}, f32[256,2048]{1,0:T(8,128)}, u32[]{:S(2)}) copy-start(f32[256,2048]{1,0:T(8,128)} %param.6) | copy-start | bytes 6291460
  299.5 4.0 %copy-start.3 = (s32[48,2]{0,1:T(2,128)S(1)}, s32[48,2]{0,1:T(2,128)}, u32[]{:S(2)}) copy-start(s32[48,2]{0,1:T(2,128)} %param.7) | copy-start | bytes 1156
  299.5 4.0 %copy-start.2 = (f32[200]{0:T(256)S(1)}, f32[200]{0:T(256)}, u32[]{:S(2)}) copy-start(f32[200]{0:T(256)} %param.8) | copy-start | bytes 2404
  299.5 74.0 %all-to-all-start.2 = ((f32[48,8,2048]{2,0,1:T(8,128)}), f32[48,8,2048]{2,0,1:T(8,128)S(1)}, u32[]{:S(2)}, u32[]{:S(2)}) async-start(f32[48,8,2048]{2,0,1:T(8,128)} %fusion), calls=%async_computation.2 | async-start | bytes 6291456 | tf_op jit(solution)/shard_map/all_to_all | solution.py:32
  303.5 70.2 %copy-start.1 = (f32[2048]{0:T(1024)S(1)}, f32[2048]{0:T(1024)}, u32[]{:S(2)}) copy-start(f32[2048]{0:T(1024)} %param.9) | copy-start | bytes 24580
